TPU v7x, 256 devices: a whole 4x4x8 slice. The times are simulated.
256 devices in a mesh: prow: 8 (over z_lo, y), pcol: 32 (over z_hi, x, core).
Axes of the slice: x: 4, y: 4, z: 8 (z_hi: 4, z_lo: 2; z = z_hi * 2 + z_lo), core: 2. Of those that a mesh axis runs over, the one named last changes fastest.
Arguments:
- matrix: bfloat16 [4096, 65536], P('prow', 'pcol'), may hold values from -6 to 6
- pivot_order: int32 [2, 4096], replicated, may hold values from 0 to 4095, as said below
- lower_inverse: float32 [2, 512, 512], replicated, as said below
- upper_inverse: float32 [2, 512, 512], replicated, as said below
Outputs:
- factored: bfloat16 [4096, 65536], P('prow', 'pcol')
Inputs may be any that keep to these rules, and one draw needn't show every extreme that they name: pivot_order[k] is a permutation, the product of 512 row swaps, the i-th exchanging row k * 512 + i with a row at or below it. It keeps every row above k * 512 in place, and every row at or below (k + 1) * 512 either stays or takes a row of rows k * 512 to (k + 1) * 512 - 1. lower_inverse[k] is unit lower triangular. upper_inverse[k] is upper triangular with a positive diagonal.
All inputs are finite; a program needn't handle non-finite values.
Results may differ from a plain program's by a relative error of at most 0.0085.
Values may be sent and summed in bfloat16 or wider, within the bound.
A program may use at most 128 MiB of HBM per device.

v0:
```python
import jax
import jax.numpy as jnp
from jax import lax
from jax.sharding import Mesh
from jax.sharding import PartitionSpec as P

NB = 512
STEPS = 2
PCOL = ("pcol_0", "pcol_1", "pcol_2")


def padded_to(lines, length):
    spare = -lines.shape[0] % length
    if not spare:
        return lines
    return jnp.concatenate([lines, jnp.zeros((spare, *lines.shape[1:]), lines.dtype)])


def broadcast_by_parts(x, axis, root):
    lines = jnp.where(lax.axis_index(axis) == root, x, jnp.zeros_like(x)).reshape(
        -1, *x.shape[1:][-1:]
    )
    padded = padded_to(lines, lax.axis_size(axis))
    own = lax.psum_scatter(padded, axis, scatter_dimension=0, tiled=True)
    return lax.all_gather(own, axis, axis=0, tiled=True)[: len(lines)].reshape(x.shape)


def cut_along(x, dim, length):
    before, after = (x.shape[:dim], x.shape[dim + 1 :])
    return jnp.moveaxis(x.reshape(*before, length, -1, *after), dim, 0)


def summed_on_arrival(x, axis, dim):
    length = lax.axis_size(axis)
    pieces = lax.all_to_all(cut_along(x, dim, length), axis, 0, 0, tiled=True)
    return jnp.sum(pieces.astype(jnp.float32), axis=0)


def laid_out(pieces, dim):
    pieces = jnp.moveaxis(pieces, 0, dim)
    dims = pieces.shape
    return pieces.reshape(*dims[:dim], dims[dim] * dims[dim + 1], *dims[dim + 2 :])


def sent_to_all(x, axis):
    length = lax.axis_size(axis)
    return lax.all_to_all(jnp.broadcast_to(x[None], (length, *x.shape)), axis, 0, 0, tiled=True)


def gather_directly(x, axis, dim):
    return laid_out(sent_to_all(x, axis), dim)


def sum_by_axis(x, axes, dim):
    far, near = axes
    own = summed_on_arrival(cut_along(x, dim, lax.axis_size(far)), near, dim + 1)
    return jnp.sum(
        lax.all_to_all(own.astype(jnp.bfloat16), far, 0, 0, tiled=True).astype(jnp.float32), axis=0
    )


def whole_of(x, axes, dim):
    far, near = axes
    initial = sent_to_all(x, far)
    pieces = jnp.swapaxes(sent_to_all(initial, near), 0, 1)
    return laid_out(pieces.reshape(-1, *x.shape), dim)


def total_of(x, axes):
    lines = x.reshape(-1, x.shape[-1])
    own = sum_by_axis(padded_to(lines, lax.axis_size(axes[0]) * lax.axis_size(axes[1])), axes, 0)
    whole = whole_of(own.astype(jnp.bfloat16), axes, 0)
    return whole[: len(lines)].reshape(x.shape).astype(jnp.float32)


def on_device(matrix, pivot_order, lower_inverse, upper_inverse):
    rows_per = lax.axis_size("prow")
    cols_per = lax.axis_size(PCOL)
    my_prow = lax.axis_index("prow")
    my_pcol = lax.axis_index(PCOL)
    local_rows, local_cols = matrix.shape
    row_slots = jnp.arange(local_rows, dtype=jnp.int32)
    col_slots = jnp.arange(local_cols, dtype=jnp.int32)
    logical_rows = (row_slots // NB * rows_per + my_prow) * NB + row_slots % NB
    logical_cols = (col_slots // NB * cols_per + my_pcol) * NB + col_slots % NB
    current = matrix
    for step_index in range(STEPS):
        top_begin = step_index * NB
        top_end = top_begin + NB
        row_order = pivot_order[step_index]
        chosen = row_order[top_begin:top_end]
        holder = chosen // NB % rows_per
        local_place = chosen // NB // rows_per * NB + chosen % NB
        picked = jnp.take(current, jnp.clip(local_place, 0, local_rows - 1), axis=0)
        selected = jnp.where((holder == my_prow)[:, None], picked, jnp.zeros_like(picked)).astype(
            jnp.float32
        )
        top_start = step_index // rows_per * NB
        root_row = step_index % rows_per
        displaced = broadcast_by_parts(current, "prow", root_row)
        source = jnp.take(row_order, logical_rows)
        from_top = (source >= top_begin) & (source < top_end) & (logical_rows >= top_end)
        moved_rows = jnp.take(displaced, jnp.clip(source - top_begin, 0, NB - 1), axis=0)
        current = jnp.where(from_top[:, None], moved_rows, current)
        top_share = summed_on_arrival(selected.astype(jnp.bfloat16), "prow", 1).astype(jnp.bfloat16)
        share_width = top_share.shape[1]
        share_cols = lax.dynamic_slice_in_dim(logical_cols, my_prow * share_width, share_width)
        solved = jnp.dot(
            lower_inverse[step_index],
            top_share.astype(jnp.float32),
            precision=lax.Precision.HIGHEST,
        ).astype(jnp.bfloat16)
        final_share = jnp.where((share_cols >= top_end)[None, :], solved, top_share)
        final_top = gather_directly(final_share, "prow", 1)
        with_top = current.at[top_start : top_start + NB].set(final_top)
        current = jnp.where(my_prow == root_row, with_top, current)
        panel_start = step_index // cols_per * NB
        root_col = step_index % cols_per
        panel_cols = current[:, panel_start : panel_start + NB]
        below = (logical_rows >= top_end)[:, None]
        is_root = my_pcol == root_col
        factor = jnp.dot(
            panel_cols.astype(jnp.float32),
            upper_inverse[step_index],
            precision=lax.Precision.HIGHEST,
        ).astype(jnp.bfloat16)
        own_part = jnp.where(
            is_root, jnp.where(below, factor, panel_cols), jnp.zeros_like(panel_cols)
        ).astype(jnp.float32)
        column = total_of(own_part.astype(jnp.bfloat16), (("pcol_0", "pcol_1"), "pcol_2")).astype(
            jnp.bfloat16
        )
        product = jnp.dot(column, final_top, preferred_element_type=jnp.float32)
        updated = (current.astype(jnp.float32) - product).astype(jnp.bfloat16)
        current = jnp.where(below & (logical_cols >= top_end)[None, :], updated, current)
        with_panel = current.at[:, panel_start : panel_start + NB].set(column)
        current = jnp.where(is_root, with_panel, current)
    return current


def solution(mesh):
    split = Mesh(
        mesh.devices.reshape(mesh.shape["prow"], 4, 4, 2), ("prow", "pcol_0", "pcol_1", "pcol_2")
    )
    return jax.shard_map(
        on_device,
        mesh=split,
        in_specs=(P("prow", PCOL), P(), P(), P()),
        out_specs=P("prow", PCOL),
        check_vma=False,
    )
```

profile of v0, /device:TPU:32, one launch (start us, length us, event | category | flops | bytes accessed | tf_op | source)
XLA Modules:
  0.0 375.6 jit_solution(4870157767368367289)
XLA Ops:
  6.5 1.5 broadcast_select_fusion
  8.1 1.5 copy-done
  9.6 3.3 gather_fusion
  12.9 1.9 select_select_fusion.3
  14.8 1.5 copy.48
  16.3 7.7 %all-to-all-start = ((bf16[8,512,256]{2,1,0:T(8,128)(2,1)}), bf16[8,512,256]{2,1,0:T(8,128)(2,1)}, u32[]{:S(2)}, u32[]{:S(2)}) async-start(bf16[8,512,256]{2,1,0:T(8,128)(2,1)} %bitcast.70), calls=%async_computation | async-start | bytes 4194304 | tf_op jit(solution)/shard_map/all_to_all | solution.py:35
  24.0 35.2 %all-to-all-done = bf16[8,512,256]{2,1,0:T(8,128)(2,1)} async-done(((bf16[8,512,256]{2,1,0:T(8,128)(2,1)}), bf16[8,512,256]{2,1,0:T(8,128)(2,1)}, u32[]{:S(2)}, u32[]{:S(2)}) %all-to-all-start) | async-done | bytes 2097184 | tf_op jit(solution)/shard_map/all_to_all | solution.py:35
  59.2 2.0 reduce_sum.72
  61.4 2.0 fusion.9
  63.5 1.5 broadcast_in_dim.114
  65.0 6.6 %all-to-all-start.1 = ((bf16[8,512,256]{2,1,0:T(8,128)(2,1)}), bf16[8,512,256]{2,1,0:T(8,128)(2,1)}, u32[]{:S(2)}, u32[]{:S(2)}) async-start(bf16[8,512,256]{2,1,0:T(8,128)(2,1)} %broadcast_in_dim.114), calls=%async_computation.1 | async-start | bytes 4194304 | tf_op jit(solution)/shard_map/all_to_all | solution.py:47
  71.6 6.2 %reduce-scatter.3.cloned.1.call-done = bf16[64,2048]{1,0:T(8,128)(2,1)} async-done(((bf16[512,2048]{1,0:T(8,128)(2,1)}), bf16[64,2048]{1,0:T(8,128)(2,1)}) %reduce-scatter.3.cloned.1.call-update) | async-done | bytes 262160 | tf_op jit(solution)/shard_map/reduce_scatter | solution.py:24
  77.9 3.1 gather_fusion.1
  81.1 12.7 %all-to-all-done.1 = bf16[8,512,256]{2,1,0:T(8,128)(2,1)} async-done(((bf16[8,512,256]{2,1,0:T(8,128)(2,1)}), bf16[8,512,256]{2,1,0:T(8,128)(2,1)}, u32[]{:S(2)}, u32[]{:S(2)}) %all-to-all-start.1) | async-done | bytes 2097184 | tf_op jit(solution)/shard_map/all_to_all | solution.py:47
  93.8 3.2 copy.41
  97.0 30.9 %all-gather.3.cloned.1.call-done = bf16[512,2048]{1,0:T(8,128)(2,1)} async-done(((bf16[64,2048]{1,0:T(8,128)(2,1)}), bf16[512,2048]{1,0:T(8,128)(2,1)}) %all-gather.3.cloned.1.call-update) | async-done | bytes 2097168 | tf_op jit(solution)/shard_map/all_gather | solution.py:25
  127.9 7.1 %gather_fusion.2 = bf16[512,2048]{1,0:T(8,128)(2,1)} fusion(bf16[512,2048]{1,0:T(8,128)(2,1)} %all-gather.3.cloned.1.call-done, s32[1024]{0:T(1024)S(1)} %pad_clamp_fusion.2), kind=kCustom, calls=%fused_computation.2.clone | custom fusion | bytes 4196352 | tf_op jit(solution)/shard_map/jit(_take)/gather | solution.py:103
  135.0 2.1 fusion.1
  137.1 1.3 copy-done.2
  138.4 1.1 fusion.4
  139.6 4.2 %all_to_all.60 = bf16[2,16,16,512]{3,2,1,0:T(8,128)(2,1)S(1)} all-to-all(bf16[2,16,16,512]{3,2,1,0:T(8,128)(2,1)S(1)} %bitcast.72), channel_id=1, replica_groups=mesh['prow'=8,'pcol_0'=4,'pcol_1'=4,'pcol_2'=2] {'pcol_2'}, dimensions={0} | all-to-all | bytes 1048576 | tf_op jit(solution)/shard_map/all_to_all | solution.py:35
  143.8 21.8 %all_to_all.61 = bf16[16,16,512]{2,1,0:T(8,128)(2,1)S(1)} all-to-all(bf16[16,16,512]{2,1,0:T(8,128)(2,1)S(1)} %reduce_sum.73), channel_id=1, replica_groups=mesh['prow'=8,'pcol_0'=4,'pcol_1'=4,'pcol_2'=2] {'pcol_0','pcol_1'}, dimensions={0} | all-to-all | bytes 524288 | tf_op jit(solution)/shard_map/all_to_all | solution.py:58
  166.4 3.7 all-to-all-start.4
  170.9 11.4 %all-to-all-done.4 = bf16[16,16,512]{2,1,0:T(8,128)(2,1)S(1)} async-done(((bf16[16,16,512]{2,1,0:T(8,128)(2,1)}), bf16[16,16,512]{2,1,0:T(8,128)(2,1)S(1)}, u32[]{:S(2)}, u32[]{:S(2)}) %all-to-all-start.4) | async-done | bytes 262176 | tf_op jit(solution)/shard_map/all_to_all | solution.py:47
  182.3 4.2 %all_to_all.62 = bf16[2,16,16,512]{3,2,1,0:T(8,128)(2,1)S(1)} all-to-all(bf16[2,16,16,512]{3,2,1,0:T(8,128)(2,1)S(1)} %broadcast_in_dim.118), channel_id=1, replica_groups=mesh['prow'=8,'pcol_0'=4,'pcol_1'=4,'pcol_2'=2] {'pcol_2'}, dimensions={0} | all-to-all | bytes 1048576 | tf_op jit(solution)/shard_map/all_to_all | solution.py:47
  186.5 4.5 %and_select_fusion = bf16[512,2048]{1,0:T(8,128)(2,1)S(1)} fusion(bf16[512,2048]{1,0:T(8,128)(2,1)} %copy-done.2, bf16[512,512]{1,0:T(8,128)(2,1)S(1)} %bitcast.78, bf16[512,2048]{1,0:T(8,128)(2,1)} %bitcast.65, pred[2048]{0:T(1024)(128)(4,1)S(1)} %broadcast_compare_fusion.1, pred[512]{0:T(512)(128)(4,1)S(1)} %broadcast_compare_fusion.3), kind=kOutput, calls=%fused_computation.8 | convolution fusion | flops 1078984704 | bytes 6818304 | tf_op jit(solution)/shard_map/dot_general | solution.py:133
  191.9 3.3 gather_fusion.3
  195.2 1.5 broadcast_select_fusion.1
  196.7 1.9 select_select_fusion.1
  198.7 43.9 %all_to_all.63 = bf16[8,512,256]{2,1,0:T(8,128)(2,1)} all-to-all(bf16[8,512,256]{2,1,0:T(8,128)(2,1)S(1)} %bitcast.71), channel_id=1, replica_groups=mesh['prow'=8,'pcol_0'=4,'pcol_1'=4,'pcol_2'=2] {'prow'}, dimensions={0} | all-to-all | bytes 4194304 | tf_op jit(solution)/shard_map/all_to_all | solution.py:35
  242.6 2.0 reduce_sum.75
  244.8 2.0 fusion.8
  246.9 1.5 broadcast_in_dim.119
  248.4 5.5 %all-to-all-start.7 = ((bf16[8,512,256]{2,1,0:T(8,128)(2,1)}), bf16[8,512,256]{2,1,0:T(8,128)(2,1)}, u32[]{:S(2)}, u32[]{:S(2)}) async-start(bf16[8,512,256]{2,1,0:T(8,128)(2,1)} %broadcast_in_dim.119), calls=%async_computation.8 | async-start | bytes 4194304 | tf_op jit(solution)/shard_map/all_to_all | solution.py:47
  254.4 3.1 gather_fusion.4
  257.6 28.8 %all-to-all-done.7 = bf16[8,512,256]{2,1,0:T(8,128)(2,1)} async-done(((bf16[8,512,256]{2,1,0:T(8,128)(2,1)}), bf16[8,512,256]{2,1,0:T(8,128)(2,1)}, u32[]{:S(2)}, u32[]{:S(2)}) %all-to-all-start.7) | async-done | bytes 2097184 | tf_op jit(solution)/shard_map/all_to_all | solution.py:47
  286.5 3.2 copy.42
  289.7 16.0 %all-gather.5.cloned.1.call-done = bf16[512,2048]{1,0:T(8,128)(2,1)} async-done(((bf16[64,2048]{1,0:T(8,128)(2,1)}), bf16[512,2048]{1,0:T(8,128)(2,1)}) %all-gather.5.cloned.1.call-update) | async-done | bytes 2097168 | tf_op jit(solution)/shard_map/all_gather | solution.py:25
  305.7 7.1 %gather_fusion.5 = bf16[512,2048]{1,0:T(8,128)(2,1)} fusion(bf16[512,2048]{1,0:T(8,128)(2,1)} %all-gather.5.cloned.1.call-done, s32[1024]{0:T(1024)S(1)} %pad_clamp_fusion), kind=kCustom, calls=%fused_computation.4.clone | custom fusion | bytes 4196352 | tf_op jit(solution)/shard_map/jit(_take)/gather | solution.py:103
  312.8 2.1 fusion
  314.9 1.3 copy-done.3
  317.4 4.2 %all_to_all.64 = bf16[2,16,16,512]{3,2,1,0:T(8,128)(2,1)S(1)} all-to-all(bf16[2,16,16,512]{3,2,1,0:T(8,128)(2,1)S(1)} %bitcast.74), channel_id=1, replica_groups=mesh['prow'=8,'pcol_0'=4,'pcol_1'=4,'pcol_2'=2] {'pcol_2'}, dimensions={0} | all-to-all | bytes 1048576 | tf_op jit(solution)/shard_map/all_to_all | solution.py:35
  321.7 18.9 %all_to_all.65 = bf16[16,16,512]{2,1,0:T(8,128)(2,1)S(1)} all-to-all(bf16[16,16,512]{2,1,0:T(8,128)(2,1)S(1)} %reduce_sum.76), channel_id=1, replica_groups=mesh['prow'=8,'pcol_0'=4,'pcol_1'=4,'pcol_2'=2] {'pcol_0','pcol_1'}, dimensions={0} | all-to-all | bytes 524288 | tf_op jit(solution)/shard_map/all_to_all | solution.py:58
  341.3 3.7 all-to-all-start.10
  345.0 12.0 %all-to-all-done.10 = bf16[16,16,512]{2,1,0:T(8,128)(2,1)S(1)} async-done(((bf16[16,16,512]{2,1,0:T(8,128)(2,1)}), bf16[16,16,512]{2,1,0:T(8,128)(2,1)S(1)}, u32[]{:S(2)}, u32[]{:S(2)}) %all-to-all-start.10) | async-done | bytes 262176 | tf_op jit(solution)/shard_map/all_to_all | solution.py:47
  357.1 4.2 %all_to_all.66 = bf16[2,16,16,512]{3,2,1,0:T(8,128)(2,1)S(1)} all-to-all(bf16[2,16,16,512]{3,2,1,0:T(8,128)(2,1)S(1)} %broadcast_in_dim.123), channel_id=1, replica_groups=mesh['prow'=8,'pcol_0'=4,'pcol_1'=4,'pcol_2'=2] {'pcol_2'}, dimensions={0} | all-to-all | bytes 1048576 | tf_op jit(solution)/shard_map/all_to_all | solution.py:47
  361.3 5.2 %and_select_fusion.1 = bf16[512,2048]{1,0:T(8,128)(2,1)} fusion(bf16[512,2048]{1,0:T(8,128)(2,1)} %copy-done.3, bf16[512,512]{1,0:T(8,128)(2,1)S(1)} %bitcast.76, bf16[512,2048]{1,0:T(8,128)(2,1)S(1)} %bitcast.67, pred[2048]{0:T(1024)(128)(4,1)S(1)} %broadcast_compare_fusion, pred[512]{0:T(512)(128)(4,1)S(1)} %broadcast_compare_fusion.2), kind=kOutput, calls=%fused_computation.9 | convolution fusion | flops 1078984704 | bytes 6818304 | tf_op jit(solution)/shard_map/dot_general | solution.py:133
  366.5 2.6 fusion.19
  (58 shorter events, 6.2 us)
Async XLA Ops:
  6.5 71.3 %reduce-scatter.3.cloned.1.call-start = ((), (), s32[]{:S(2)}) async-start(), calls=%async_computation.14 | async-start | bytes 2359296 | tf_op jit(solution)/shard_map/reduce_scatter | solution.py:24
  6.5 1.5 copy-start.4
  8.0 1.6 copy-start
  16.3 43.0 %all-to-all-start = ((bf16[8,512,256]{2,1,0:T(8,128)(2,1)}), bf16[8,512,256]{2,1,0:T(8,128)(2,1)}, u32[]{:S(2)}, u32[]{:S(2)}) async-start(bf16[8,512,256]{2,1,0:T(8,128)(2,1)} %bitcast.70), calls=%async_computation | async-start | bytes 4194304 | tf_op jit(solution)/shard_map/all_to_all | solution.py:35
  65.0 28.8 %all-to-all-start.1 = ((bf16[8,512,256]{2,1,0:T(8,128)(2,1)}), bf16[8,512,256]{2,1,0:T(8,128)(2,1)}, u32[]{:S(2)}, u32[]{:S(2)}) async-start(bf16[8,512,256]{2,1,0:T(8,128)(2,1)} %broadcast_in_dim.114), calls=%async_computation.1 | async-start | bytes 4194304 | tf_op jit(solution)/shard_map/all_to_all | solution.py:47
  71.6 56.3 %all-gather.3.cloned.1.call-start = ((), (), s32[]{:S(2)}) async-start(), calls=%async_computation.15 | async-start | bytes 2359296 | tf_op jit(solution)/shard_map/all_gather | solution.py:25
  135.0 3.5 copy-start.5
  137.1 1.3 copy-start.2
  166.4 15.8 %all-to-all-start.4 = ((bf16[16,16,512]{2,1,0:T(8,128)(2,1)}), bf16[16,16,512]{2,1,0:T(8,128)(2,1)S(1)}, u32[]{:S(2)}, u32[]{:S(2)}) async-start(bf16[16,16,512]{2,1,0:T(8,128)(2,1)} %broadcast_in_dim.117), calls=%async_computation.5 | async-start | bytes 524288 | tf_op jit(solution)/shard_map/all_to_all | solution.py:47
  170.1 83.8 %reduce-scatter.5.cloned.1.call-start = ((), (), s32[]{:S(2)}) async-start(), calls=%async_computation.16 | async-start | bytes 2359296 | tf_op jit(solution)/shard_map/reduce_scatter | solution.py:24
  248.4 38.1 %all-to-all-start.7 = ((bf16[8,512,256]{2,1,0:T(8,128)(2,1)}), bf16[8,512,256]{2,1,0:T(8,128)(2,1)}, u32[]{:S(2)}, u32[]{:S(2)}) async-start(bf16[8,512,256]{2,1,0:T(8,128)(2,1)} %broadcast_in_dim.119), calls=%async_computation.8 | async-start | bytes 4194304 | tf_op jit(solution)/shard_map/all_to_all | solution.py:47
  253.9 51.8 %all-gather.5.cloned.1.call-start = ((), (), s32[]{:S(2)}) async-start(), calls=%async_computation.17 | async-start | bytes 2359296 | tf_op jit(solution)/shard_map/all_gather | solution.py:25
  312.8 3.5 copy-start.6
  314.9 1.3 copy-start.3
  340.6 20.7 %copy-start.1 = (bf16[8,64,8,256]{3,2,0,1:T(8,128)(2,1)S(1)}, bf16[8,64,8,256]{3,2,0,1:T(8,128)(2,1)}, u32[]{:S(2)}) copy-start(bf16[8,64,8,256]{3,2,0,1:T(8,128)(2,1)} %copy.42) | copy-start | bytes 6291460
  341.3 15.7 %all-to-all-start.10 = ((bf16[16,16,512]{2,1,0:T(8,128)(2,1)}), bf16[16,16,512]{2,1,0:T(8,128)(2,1)S(1)}, u32[]{:S(2)}, u32[]{:S(2)}) async-start(bf16[16,16,512]{2,1,0:T(8,128)(2,1)} %broadcast_in_dim.122), calls=%async_computation.12 | async-start | bytes 524288 | tf_op jit(solution)/shard_map/all_to_all | solution.py:47
Sparse Core Ops, SparseCore 0:
  9.9 67.8 reduce-scatter.2
  79.6 48.2 all-gather.2
  196.8 56.5 reduce-scatter.4
  256.1 49.5 all-gather.4
where the time goes:
time: 379 us; the launch traced here: 376 us
  waiting for transfers between devices  154 us (41%)
  blocking collectives  101 us (27%)
  local copies, waits for them, and re-layouts  44.4 us (12%)
  starting transfers between devices  27.2 us (7%)
  other arithmetic  19.7 us (5%)
  matrix products  15.8 us (4%)
  between operations  13.5 us (4%)
    all_to_all x4, waiting for transfers between devices, sent_to_all(): lax.all_to_all(jnp.broadcast_to(x[None], (length, *x.shape)), axis, 0, 0,...  64.9 us
    all_to_all x3, blocking collectives, summed_on_arrival(): pieces = lax.all_to_all(cut_along(x, dim, length), axis, 0, 0, tiled=True)  52.2 us
    all_gather x2, waiting for transfers between devices, broadcast_by_parts(): lax.all_gather(own, axis, axis=0, tiled=True)[:len(lines)].reshape(x.shape)  46.9 us
    all_to_all x2, blocking collectives, sum_by_axis(): lax.all_to_all(own.astype(jnp.bfloat16), far, 0, 0, tiled=True)  40.7 us
    all_to_all x1, waiting for transfers between devices, summed_on_arrival(): pieces = lax.all_to_all(cut_along(x, dim, length), axis, 0, 0, tiled=True)  35.2 us
    all_to_all x4, starting transfers between devices, sent_to_all(): lax.all_to_all(jnp.broadcast_to(x[None], (length, *x.shape)), axis, 0, 0,...  19.5 us
    gather x2, local copies, waits for them, and re-layouts, on_device(): jnp.take(displaced, jnp.clip(source - top_begin, 0, NB - 1), axis=0)  14.2 us
    dot_general x2, matrix products, on_device(): product = jnp.dot(column, final_top, preferred_element_type=jnp.float32)  9.7 us
  transfers between devices with their start and end apart: 9, of which 8 were waited for; matrix products, arithmetic and copies ran while one was open for 9% of the time, Pallas kernels for 0%

commit v1 on v0

v1 whole, which is shorter than its diff:
```python
import jax
import jax.numpy as jnp
from jax import lax
from jax.experimental import pallas as pl
from jax.experimental.pallas import tpu as pltpu
from jax.sharding import PartitionSpec as P

NB = 512
W = 256
BF, F32, I32 = jnp.bfloat16, jnp.float32, jnp.int32
MESH = pl.DeviceIdType.MESH
NEAR = ((1, 0), (3, 0), (2, 0), (0, 1))
FAR = ((1, 1), (3, 1), (2, 1))
PEERS = NEAR + FAR


def mm(a, b):
    return jnp.dot(a, b, preferred_element_type=F32)


def parts(x):
    high = x.astype(BF)
    return high, (x - high.astype(F32)).astype(BF)


def kernel(
    mat, piv, low, upp, out,
    a, raw, cur, fin, res, l0, l1, src, l0p, sel, got, top, lowv, lowh, lowl, uppv, tab, order, t32, u0, u1,
    sem_a, sem_w, sem_o, p1s, p1r, rss, rsr, ags, agr, lps, a1s, ar, a2s, bs, br, cs, cr, ds, dr, p2s, p2r,
):
    p, c = lax.axis_index("prow"), lax.axis_index("pcol")
    zl, y = p // 4, p % 4
    zh, e = c // 8, c % 8
    x, co = e // 2, e % 2
    ls = (l0, l1)

    def peer(dy, dz):
        return (zl + dz) % 2 * 4 + (y + dy) % 4

    def at_x(dx, core):
        return (x + dx) % 4 * 2 + core

    def remote(s, d, ss, rs, to):
        return pltpu.make_async_remote_copy(
            src_ref=s, dst_ref=d, send_sem=ss, recv_sem=rs, device_id=to, device_id_type=MESH
        )

    load = [
        pltpu.make_async_copy(mat.at[:, W * j : W * j + W], a.at[j], sem_a.at[j]) for j in range(8)
    ]
    for cp in load:
        cp.start()
    load_u = pltpu.make_async_copy(upp.at[c % 2], uppv, sem_w.at[0])
    load_u.start()
    load_l = pltpu.make_async_copy(low, lowv, sem_w.at[1])
    load_l.start()

    barrier = pltpu.get_barrier_semaphore()
    for d in PEERS:
        pl.semaphore_signal(barrier, inc=1, device_id=(peer(*d), c), device_id_type=MESH)
    for d in range(1, 8):
        pl.semaphore_signal(barrier, inc=1, device_id=(p, zh * 8 + (e + d) % 8), device_id_type=MESH)
    for d in range(1, 4):
        pl.semaphore_signal(barrier, inc=1, device_id=(p, (zh + d) % 4 * 8 + e), device_id_type=MESH)

    for k in range(2):
        for i in range(32):
            tab[k, i : i + 1, :] = piv[k : k + 1, 128 * i : 128 * i + 128]
    lanes = lax.broadcasted_iota(I32, (NB, 128), 1)
    rows = lax.broadcasted_iota(I32, (NB, 1), 0)

    def looked_up(k, index):
        t = tab[k]
        table = jnp.concatenate([t // 64, t % 64], axis=1).astype(F32).astype(BF)
        hot = jnp.where(lax.broadcasted_iota(I32, (NB, 32), 1) == index // 128, 1.0, 0.0).astype(BF)
        both = mm(hot, table)
        value = both[:, :128] * 64.0 + both[:, 128:]
        return jnp.sum(jnp.where(lanes == index % 128, value, 0.0), axis=1, keepdims=True).astype(I32)

    def hot_rows(index, base, n):
        return jnp.where(lax.broadcasted_iota(I32, (NB, n), 1) + base == index, 1.0, 0.0).astype(BF)

    order[0] = jnp.broadcast_to(looked_up(0, rows), (NB, 128))
    for cp in load:
        cp.wait()
    load_u.wait()
    load_l.wait()
    pl.semaphore_wait(barrier, 17)

    def send_raw(d):
        j = peer(*d)
        return remote(a.at[j], raw.at[p], p1s.at[j], p1r.at[p], (j, c))

    def scatter(k, piece):
        to = zh * 8 + piece
        return remote(src.at[piece], ls[k].at[piece, p], a1s.at[k, piece], ar.at[k], (p, to))

    def share_up(d):
        j = peer(*d)
        return remote(sel.at[j], got.at[p], rss.at[j], rsr.at[p], (j, c))

    def share_top(d):
        j = peer(*d)
        return remote(top.at[p], top.at[p], ags.at[j], agr.at[p], (j, c))

    whole = remote(src, l0p, lps.at[0], lps.at[1], (p, zh * 8 + (e + 1) % 8))

    def panel_factor(first, second):
        uh, ul = parts(uppv[...])
        acc = mm(first, uh[:W]) + mm(second, uh[W:]) + (mm(first, ul[:W]) + mm(second, ul[W:]))
        src[...] = acc.astype(BF).reshape(8, 64, NB)

    @pl.when(c == 0)
    def _():
        panel_factor(a[0], a[1])
        l0[0, p] = src[0]
        for piece in range(1, 8):
            scatter(0, piece).start()
        whole.start()

    @pl.when(c == 1)
    def _():
        hot = hot_rows(order[0, :, 0:1], p * NB, NB)
        for j in range(2):
            sel[:, :, W * j : W * j + W] = mm(hot, a[j]).astype(BF).reshape(8, 64, W)
        got[p] = sel[p]
        for d in PEERS:
            share_up(d).start()

    @pl.when(c >= 2)
    def _():
        for d in NEAR:
            send_raw(d).start()

    def copies(k):
        def up(d):
            to = (zh + d) % 4 * 8 + e
            return remote(ls[k].at[e, p], ls[k].at[e, p], a2s.at[k, d], ar.at[k], (p, to))

        def across(d):
            j = peer(*d)
            return remote(ls[k].at[e, p], ls[k].at[e, p], bs.at[k, j], br.at[k, p], (j, c))

        def over_x(h, d):
            part = ls[k].at[e, pl.ds(4 * h, 4)]
            return remote(part, part, cs.at[k, h, d], cr.at[k, h, x], (p, zh * 8 + at_x(d, co)))

        def over_core(h, d):
            s = at_x(d, co)
            part = ls[k].at[s, pl.ds(4 * h, 4)]
            return remote(part, part, ds.at[k, h, d], dr.at[k, h, s // 2], (p, zh * 8 + at_x(0, 1 - co)))

        def got_x(h, d):
            s = at_x(d, co)
            part = ls[k].at[s, pl.ds(4 * h, 4)]
            return remote(part, part, cs.at[k, h, d], cr.at[k, h, s // 2], (p, zh * 8 + s))

        def got_core(h, d):
            s = at_x(d, 1 - co)
            part = ls[k].at[s, pl.ds(4 * h, 4)]
            return remote(part, part, ds.at[k, h, d], dr.at[k, h, s // 2], (p, zh * 8 + at_x(0, 1 - co)))

        def got_p(d):
            j = peer(*d)
            part = ls[k].at[e, j]
            return remote(part, part, bs.at[k, j], br.at[k, j], (j, c))

        return up, across, over_x, over_core, got_x, got_core, got_p

    kit = (copies(0), copies(1))

    def pass_piece(k):
        up, across = kit[k][:2]

        @pl.when(c != k)
        def _():
            part = ls[k].at[e, p]
            remote(part, part, a1s.at[k, 0], ar.at[k], (p, zh * 8 + (e + 1) % 8)).wait_recv()

        @pl.when(zh == 0)
        def _():
            for d in range(1, 4):
                up(d).start()

        for d in PEERS:
            across(d).start()

    def pass_block(k):
        _, _, over_x, over_core, _, _, got_p = kit[k]
        for d in PEERS:
            got_p(d).wait_recv()
        for h in range(2):
            for d in (1, 3, 2):
                over_x(h, d).start()
            over_core(h, 0).start()

    def take_half(k, h):
        _, _, _, over_core, got_x, got_core, _ = kit[k]
        for d in (1, 3, 2):
            got_x(h, d).wait_recv()
            over_core(h, d).start()
        for d in range(4):
            got_core(h, d).wait_recv()

    pass_piece(0)

    lowh[...] = lowv[...].astype(BF)
    lowl[...] = (lowv[...] - lowh[...].astype(F32)).astype(BF)

    @pl.when(c == 1)
    def _():
        for d in PEERS:
            j = peer(*d)
            remote(sel.at[j], got.at[j], rss.at[j], rsr.at[j], (j, c)).wait_recv()
        total = got[0].astype(F32)
        for j in range(1, 8):
            total = total + got[j].astype(F32)
        top[p] = total.astype(BF)
        for d in PEERS:
            share_top(d).start()
        for d in PEERS:
            j = peer(*d)
            remote(top.at[j], top.at[j], ags.at[j], agr.at[j], (j, c)).wait_recv()
        remote(src, l0p, lps.at[0], lps.at[1], (p, zh * 8 + (e + 7) % 8)).wait_recv()
        tops = top[...].reshape(NB, NB)
        solved = (mm(lowh[0], tops) + mm(lowl[0], tops)).astype(BF)
        less = mm(l0p[...].reshape(NB, NB), solved)
        first = (a[0].astype(F32) - less[:, :W]).astype(BF)
        second = (a[1].astype(F32) - less[:, W:]).astype(BF)
        panel_factor(first, second)
        l1[1, p] = src[1]
        for piece in (0, 2, 3, 4, 5, 6, 7):
            scatter(1, piece).start()

    @pl.when(c < 2)
    def _():
        for d in NEAR:
            send_raw(d).start()

    for d in FAR:
        send_raw(d).start()

    raw[p] = a[p]
    both = jnp.zeros((NB, 128), I32)
    for q in range(1, 8):
        both = jnp.where(lanes == q, looked_up(0, looked_up(1, rows + NB * q)), both)
    order[1] = both

    pass_block(0)
    pass_piece(1)

    for d in PEERS:
        j = peer(*d)
        remote(a.at[j], raw.at[j], p1s.at[j], p1r.at[j], (j, c)).wait_recv()

    def picked(index, ref):
        t32[...] = jnp.zeros((NB, W), F32)

        def add(q, _):
            t32[...] += mm(hot_rows(index, q * NB, NB), ref[q])
            return 0

        lax.fori_loop(0, 8, add, 0)
        return t32[...].astype(BF)

    def solved_by(k, t):
        return (mm(lowh[k], t) + mm(lowl[k], t)).astype(BF)

    own0 = jnp.where(c == 0, 1, 0) * jnp.where(p < 2, 1, 0)
    own1 = jnp.where(c == 1, 1, 0) * jnp.where(p < 2, 1, 0)
    cols = pl.ds(pl.multiple_of(p % 2 * W, W), W)

    t0 = picked(order[0, :, 0:1], raw)
    u0[...] = solved_by(0, t0)

    @pl.when(own0 == 1)
    def _():
        fin[0] = t0

    @pl.when(own0 == 0)
    def _():
        fin[0] = u0[...]

    def send_done(q):
        return remote(fin.at[q], res.at[p], p2s.at[q], p2r.at[p], (q, c))

    def finish(q):
        @pl.when(p == q)
        def _():
            res[q] = fin[q]

        @pl.when(p != q)
        def _():
            send_done(q).start()

    finish(0)
    pass_block(1)
    for h in range(2):
        take_half(0, h)

        def update(q, _):
            @pl.when(own0 == 0)
            def _():
                less = mm(l0[:, q].reshape(NB, NB), u0[...])
                cur[q] = (raw[q].astype(F32) - less).astype(BF)

            @pl.when(own0 == 1)
            def _():
                cur[q] = l0[:, q, :, cols].reshape(NB, W)

            return 0

        lax.fori_loop(4 * h, 4 * h + 4, update, 0)

    t1 = picked(order[1, :, 1:2], cur)
    u1[...] = solved_by(1, t1)

    @pl.when(own0 + own1 == 1)
    def _():
        fin[1] = t1

    @pl.when(own0 + own1 == 0)
    def _():
        fin[1] = u1[...]

    finish(1)
    for h in range(2):
        take_half(1, h)

        def update_again(q, _):
            @pl.when(own0 + own1 == 0)
            def _():
                less = mm(l1[:, q].reshape(NB, NB), u1[...])
                cur[q] = (cur[q].astype(F32) - less).astype(BF)

            @pl.when(own1 == 1)
            def _():
                cur[q] = l1[:, q, :, cols].reshape(NB, W)

            return 0

        lax.fori_loop(4 * h, 4 * h + 4, update_again, 0)
        for q in range(max(4 * h, 2), 4 * h + 4):
            index = order[1, :, q : q + 1]
            moved = mm(hot_rows(index, 0, NB), cur[0]) + mm(hot_rows(index, NB, NB), cur[1])
            fin[q] = jnp.where(index < 2 * NB, moved, cur[q].astype(F32)).astype(BF)
            finish(q)

    def store(j):
        return pltpu.make_async_copy(res.at[j], out.at[:, pl.ds(pl.multiple_of(j * W, W), W)], sem_o.at[j])

    store(p).start()
    for d in PEERS:
        j = peer(*d)
        remote(fin.at[j], res.at[j], p2s.at[j], p2r.at[j], (j, c)).wait_recv()
        store(j).start()

    for d in PEERS:
        send_raw(d).wait_send()
        send_done(peer(*d)).wait_send()
    for k in range(2):
        up, across, over_x, over_core, _, _, _ = kit[k]

        @pl.when(c == k)
        def _():
            for piece in range(8):
                if piece != k:
                    scatter(k, piece).wait_send()

        @pl.when(zh == 0)
        def _():
            for d in range(1, 4):
                up(d).wait_send()

        for d in PEERS:
            across(d).wait_send()
        for h in range(2):
            for d in (1, 3, 2):
                over_x(h, d).wait_send()
            for d in range(4):
                over_core(h, d).wait_send()

    @pl.when(c == 0)
    def _():
        whole.wait_send()

    @pl.when(c == 1)
    def _():
        for d in PEERS:
            share_up(d).wait_send()
            share_top(d).wait_send()

    store(p).wait()
    for d in PEERS:
        store(peer(*d)).wait()


def on_device(matrix, pivot_order, lower_inverse, upper_inverse):
    any_space = pl.BlockSpec(memory_space=pl.ANY)
    dma = pltpu.SemaphoreType.DMA
    shares = pltpu.VMEM((8, NB, W), BF)
    pieces = pltpu.VMEM((8, 64, NB), BF)
    return pl.pallas_call(
        kernel,
        out_shape=jax.ShapeDtypeStruct(matrix.shape, matrix.dtype),
        in_specs=[any_space, pl.BlockSpec(memory_space=pltpu.VMEM), any_space, any_space],
        out_specs=any_space,
        scratch_shapes=[
            shares, shares, shares, shares, shares,
            pltpu.VMEM((8, 8, 64, NB), BF), pltpu.VMEM((8, 8, 64, NB), BF),
            pieces, pieces, pieces, pieces, pieces,
            pltpu.VMEM((2, NB, NB), F32), pltpu.VMEM((2, NB, NB), BF), pltpu.VMEM((2, NB, NB), BF),
            pltpu.VMEM((NB, NB), F32), pltpu.VMEM((2, 32, 128), I32), pltpu.VMEM((2, NB, 128), I32),
            pltpu.VMEM((NB, W), F32), pltpu.VMEM((NB, W), BF), pltpu.VMEM((NB, W), BF),
            dma((8,)), dma((2,)), dma((8,)),
            dma((8,)), dma((8,)), dma((8,)), dma((8,)), dma((8,)), dma((8,)), dma((2,)),
            dma((2, 8)), dma((2,)), dma((2, 4)), dma((2, 8)), dma((2, 8)),
            dma((2, 2, 4)), dma((2, 2, 4)), dma((2, 2, 4)), dma((2, 2, 4)), dma((8,)), dma((8,)),
        ],
        compiler_params=pltpu.CompilerParams(
            collective_id=0, has_side_effects=True, vmem_limit_bytes=60 << 20
        ),
    )(matrix, pivot_order, lower_inverse, upper_inverse)


def solution(mesh):
    return jax.shard_map(
        on_device,
        mesh=mesh,
        in_specs=(P("prow", "pcol"), P(), P(), P()),
        out_specs=P("prow", "pcol"),
        check_vma=False,
    )
```

time: 379 us -> 124 us (0.33)
  the two profiles are of different devices: /device:TPU:32 before, /device:TPU:187 now
where the time goes in v1:
time: 124 us
  Pallas kernels  121 us (98%)
  local copies, waits for them, and re-layouts  3.16 us (3%)
    pallas_call x1, Pallas kernels, on_device(): pl.pallas_call(kernel, out_shape=jax.ShapeDtypeStruct(matrix.shape, matri...  121 us
    unnamed x1, local copies, waits for them, and re-layouts  3.16 us

profile of v1, /device:TPU:187, one launch (start us, length us, event | category | flops | bytes accessed | tf_op | source)
XLA Modules:
  0.0 123.8 jit_solution(12446634233741777936)
XLA Ops:
  0.0 120.7 %shard_map.46 = bf16[512,2048]{1,0:T(8,128)(2,1)} custom-call(bf16[512,2048]{1,0:T(8,128)(2,1)} %mat.1, s32[2,4096]{1,0:T(2,128)} %piv.1, f32[2,512,512]{2,1,0:T(8,128)} %low.1, f32[2,512,512]{2,1,0:T(8,128)} %upp.1), custom_call_target="tpu_custom_call" | custom-call | tf_op jit(solution)/shard_map/pallas_call | solution.py:403
  120.7 3.2 %copy.6 = bf16[512,2048]{1,0:T(8,128)(2,1)} copy(bf16[512,2048]{1,0:T(8,128)(2,1)} %shard_map.46) | data formatting | bytes 4194304

commit v2 on v1

--- a/solution.py
+++ b/solution.py
@@ -9,9 +9,9 @@
 W = 256
 BF, F32, I32 = jnp.bfloat16, jnp.float32, jnp.int32
 MESH = pl.DeviceIdType.MESH
-NEAR = ((1, 0), (3, 0), (2, 0), (0, 1))
-FAR = ((1, 1), (3, 1), (2, 1))
-PEERS = NEAR + FAR
+WAVES = (((1, 0), (3, 0), (2, 0), (0, 1)), ((1, 1), (3, 1), (2, 1)))
+PEERS = WAVES[0] + WAVES[1]
+AROUND = (1, 3)
 
 
 def mm(a, b):
@@ -25,8 +25,8 @@
 
 def kernel(
     mat, piv, low, upp, out,
-    a, raw, cur, fin, res, l0, l1, src, l0p, sel, got, top, lowv, lowh, lowl, uppv, tab, order, t32, u0, u1,
-    sem_a, sem_w, sem_o, p1s, p1r, rss, rsr, ags, agr, lps, a1s, ar, a2s, bs, br, cs, cr, ds, dr, p2s, p2r,
+    a, raw, cur, fin, l0, l1, src, l0p, sel, got, top, lowv, lowh, lowl, uppv, tab, order, t32, u0, u1,
+    sem_a, sem_w, p1s, p1r, rss, rsr, ags, agr, lps, a1s, ar, a2s, bs, br, cs, cr, ds, dr, p2s, p2r,
 ):
     p, c = lax.axis_index("prow"), lax.axis_index("pcol")
     zl, y = p // 4, p % 4
@@ -129,8 +129,15 @@
 
     @pl.when(c >= 2)
     def _():
-        for d in NEAR:
+        for d in WAVES[0]:
             send_raw(d).start()
+
+    def pair(s):
+        if s == 0:
+            return 0
+        high, low_bit = p // 4, p // 2 % 2
+        other = (1 - high if s > 1 else high) * 2 + (low_bit if s == 2 else 1 - low_bit)
+        return 2 * (other + p // 2 * (1 - (other + 3) // 4))
 
     def copies(k):
         def up(d):
@@ -141,31 +148,37 @@
             j = peer(*d)
             return remote(ls[k].at[e, p], ls[k].at[e, p], bs.at[k, j], br.at[k, p], (j, c))
 
-        def over_x(h, d):
-            part = ls[k].at[e, pl.ds(4 * h, 4)]
-            return remote(part, part, cs.at[k, h, d], cr.at[k, h, x], (p, zh * 8 + at_x(d, co)))
-
-        def over_core(h, d):
-            s = at_x(d, co)
-            part = ls[k].at[s, pl.ds(4 * h, 4)]
-            return remote(part, part, ds.at[k, h, d], dr.at[k, h, s // 2], (p, zh * 8 + at_x(0, 1 - co)))
-
-        def got_x(h, d):
-            s = at_x(d, co)
-            part = ls[k].at[s, pl.ds(4 * h, 4)]
-            return remote(part, part, cs.at[k, h, d], cr.at[k, h, s // 2], (p, zh * 8 + s))
-
-        def got_core(h, d):
-            s = at_x(d, 1 - co)
-            part = ls[k].at[s, pl.ds(4 * h, 4)]
-            return remote(part, part, ds.at[k, h, d], dr.at[k, h, s // 2], (p, zh * 8 + at_x(0, 1 - co)))
-
-        def got_p(d):
-            j = peer(*d)
-            part = ls[k].at[e, j]
-            return remote(part, part, bs.at[k, j], br.at[k, j], (j, c))
-
-        return up, across, over_x, over_core, got_x, got_core, got_p
+        def block(d, core, s):
+            return ls[k].at[at_x(d, core), pl.ds(pair(s), 2)]
+
+        def row_of(d, s, i):
+            return ls[k].at[at_x(d, co), pair(s) + i]
+
+        def over_x(s, i):
+            part = block(0, co, s)
+            return remote(part, part, cs.at[k, s, i], cr.at[k, s, i], (p, zh * 8 + at_x(AROUND[i], co)))
+
+        def onward(s, i):
+            part = row_of(AROUND[1 - i], s, i)
+            return remote(part, part, cs.at[k, s, 2 + i], cr.at[k, s, 2 + i], (p, zh * 8 + at_x(AROUND[i], co)))
+
+        def over_core(s, d):
+            part = block(d, co, s)
+            return remote(part, part, ds.at[k, s, d], dr.at[k, s, d], (p, zh * 8 + at_x(0, 1 - co)))
+
+        def got_x(s, i):
+            part = block(AROUND[1 - i], co, s)
+            return remote(part, part, cs.at[k, s, i], cr.at[k, s, i], (p, zh * 8 + at_x(AROUND[i], co)))
+
+        def got_onward(s, i):
+            part = row_of(2, s, i)
+            return remote(part, part, cs.at[k, s, 2 + i], cr.at[k, s, 2 + i], (p, zh * 8 + at_x(AROUND[i], co)))
+
+        def got_core(s, d):
+            part = block(d, 1 - co, s)
+            return remote(part, part, ds.at[k, s, d], dr.at[k, s, d], (p, zh * 8 + at_x(0, 1 - co)))
+
+        return up, across, over_x, onward, over_core, got_x, got_onward, got_core
 
     kit = (copies(0), copies(1))
 
@@ -185,22 +198,34 @@
         for d in PEERS:
             across(d).start()
 
-    def pass_block(k):
-        _, _, over_x, over_core, _, _, got_p = kit[k]
-        for d in PEERS:
-            got_p(d).wait_recv()
-        for h in range(2):
-            for d in (1, 3, 2):
-                over_x(h, d).start()
-            over_core(h, 0).start()
-
-    def take_half(k, h):
-        _, _, _, over_core, got_x, got_core, _ = kit[k]
-        for d in (1, 3, 2):
-            got_x(h, d).wait_recv()
-            over_core(h, d).start()
+    def step(k, s):
+        _, _, over_x, _, over_core, _, _, _ = kit[k]
+        for i in range(2):
+            q = pair(s) + i
+
+            @pl.when(q != p)
+            def _():
+                part = ls[k].at[e, q]
+                remote(part, part, bs.at[k, q], br.at[k, q], (q, c)).wait_recv()
+
+        for i in range(2):
+            over_x(s, i).start()
+        over_core(s, 0).start()
+
+    def forward(k, s):
+        _, _, _, onward, over_core, got_x, _, _ = kit[k]
+        for i in range(2):
+            got_x(s, i).wait_recv()
+            onward(s, i).start()
+            over_core(s, AROUND[1 - i]).start()
+
+    def collect(k, s):
+        _, _, _, _, over_core, _, got_onward, got_core = kit[k]
+        for i in range(2):
+            got_onward(s, i).wait_recv()
+        over_core(s, 2).start()
         for d in range(4):
-            got_core(h, d).wait_recv()
+            got_core(s, d).wait_recv()
 
     pass_piece(0)
 
@@ -234,10 +259,10 @@
 
     @pl.when(c < 2)
     def _():
-        for d in NEAR:
+        for d in WAVES[0]:
             send_raw(d).start()
 
-    for d in FAR:
+    for d in WAVES[1]:
         send_raw(d).start()
 
     raw[p] = a[p]
@@ -246,8 +271,15 @@
         both = jnp.where(lanes == q, looked_up(0, looked_up(1, rows + NB * q)), both)
     order[1] = both
 
-    pass_block(0)
+    step(0, 0)
+    step(0, 1)
+    forward(0, 0)
+    step(0, 2)
+    forward(0, 1)
+    step(0, 3)
     pass_piece(1)
+    forward(0, 2)
+    forward(0, 3)
 
     for d in PEERS:
         j = peer(*d)
@@ -281,24 +313,19 @@
     def _():
         fin[0] = u0[...]
 
+    mine = pl.ds(pl.multiple_of(p * W, W), W)
+
     def send_done(q):
-        return remote(fin.at[q], res.at[p], p2s.at[q], p2r.at[p], (q, c))
-
-    def finish(q):
-        @pl.when(p == q)
-        def _():
-            res[q] = fin[q]
-
-        @pl.when(p != q)
-        def _():
-            send_done(q).start()
-
-    finish(0)
-    pass_block(1)
-    for h in range(2):
-        take_half(0, h)
-
-        def update(q, _):
+        return remote(fin.at[q], out.at[:, mine], p2s.at[q], p2r.at[p], (q, c))
+
+    step(1, 0)
+    step(1, 1)
+
+    def update(s):
+        collect(0, s)
+        for i in range(2):
+            q = pair(s) + i
+
             @pl.when(own0 == 0)
             def _():
                 less = mm(l0[:, q].reshape(NB, NB), u0[...])
@@ -308,10 +335,14 @@
             def _():
                 cur[q] = l0[:, q, :, cols].reshape(NB, W)
 
-            return 0
-
-        lax.fori_loop(4 * h, 4 * h + 4, update, 0)
-
+    update(0)
+    update(1)
+    forward(1, 0)
+    step(1, 2)
+    update(2)
+    update(3)
+    forward(1, 1)
+    step(1, 3)
     t1 = picked(order[1, :, 1:2], cur)
     u1[...] = solved_by(1, t1)
 
@@ -323,11 +354,11 @@
     def _():
         fin[1] = u1[...]
 
-    finish(1)
-    for h in range(2):
-        take_half(1, h)
-
-        def update_again(q, _):
+    def update_again(s):
+        collect(1, s)
+        for i in range(2):
+            q = pair(s) + (i + p) % 2
+
             @pl.when(own0 + own1 == 0)
             def _():
                 less = mm(l1[:, q].reshape(NB, NB), u1[...])
@@ -337,29 +368,33 @@
             def _():
                 cur[q] = l1[:, q, :, cols].reshape(NB, W)
 
-            return 0
-
-        lax.fori_loop(4 * h, 4 * h + 4, update_again, 0)
-        for q in range(max(4 * h, 2), 4 * h + 4):
-            index = order[1, :, q : q + 1]
-            moved = mm(hot_rows(index, 0, NB), cur[0]) + mm(hot_rows(index, NB, NB), cur[1])
-            fin[q] = jnp.where(index < 2 * NB, moved, cur[q].astype(F32)).astype(BF)
-            finish(q)
-
-    def store(j):
-        return pltpu.make_async_copy(res.at[j], out.at[:, pl.ds(pl.multiple_of(j * W, W), W)], sem_o.at[j])
-
-    store(p).start()
+            if s:
+                index = jnp.sum(
+                    jnp.where(lanes == q, order[1].astype(F32), 0.0), axis=1, keepdims=True
+                ).astype(I32)
+                moved = mm(hot_rows(index, 0, NB), cur[0]) + mm(hot_rows(index, NB, NB), cur[1])
+                fin[q] = jnp.where(index < 2 * NB, moved, cur[q].astype(F32)).astype(BF)
+
+    forward(1, 2)
+    update_again(0)
+    forward(1, 3)
+    for s in range(1, 4):
+        update_again(s)
+
+    out[:, mine] = fin[p]
+    for d in PEERS:
+        send_done(peer(*d)).start()
+
     for d in PEERS:
         j = peer(*d)
-        remote(fin.at[j], res.at[j], p2s.at[j], p2r.at[j], (j, c)).wait_recv()
-        store(j).start()
+        part = out.at[:, pl.ds(pl.multiple_of(j * W, W), W)]
+        remote(fin.at[j], part, p2s.at[j], p2r.at[j], (j, c)).wait_recv()
 
     for d in PEERS:
         send_raw(d).wait_send()
         send_done(peer(*d)).wait_send()
     for k in range(2):
-        up, across, over_x, over_core, _, _, _ = kit[k]
+        up, across, over_x, onward, over_core, _, _, _ = kit[k]
 
         @pl.when(c == k)
         def _():
@@ -374,11 +409,12 @@
 
         for d in PEERS:
             across(d).wait_send()
-        for h in range(2):
-            for d in (1, 3, 2):
-                over_x(h, d).wait_send()
+        for s in range(4):
+            for i in range(2):
+                over_x(s, i).wait_send()
+                onward(s, i).wait_send()
             for d in range(4):
-                over_core(h, d).wait_send()
+                over_core(s, d).wait_send()
 
     @pl.when(c == 0)
     def _():
@@ -389,10 +425,6 @@
         for d in PEERS:
             share_up(d).wait_send()
             share_top(d).wait_send()
-
-    store(p).wait()
-    for d in PEERS:
-        store(peer(*d)).wait()
 
 
 def on_device(matrix, pivot_order, lower_inverse, upper_inverse):
@@ -402,20 +434,20 @@
     pieces = pltpu.VMEM((8, 64, NB), BF)
     return pl.pallas_call(
         kernel,
-        out_shape=jax.ShapeDtypeStruct(matrix.shape, matrix.dtype),
+        out_shape=pltpu.VMEM(matrix.shape, matrix.dtype),
         in_specs=[any_space, pl.BlockSpec(memory_space=pltpu.VMEM), any_space, any_space],
-        out_specs=any_space,
+        out_specs=pl.BlockSpec(memory_space=pltpu.VMEM),
         scratch_shapes=[
-            shares, shares, shares, shares, shares,
+            shares, shares, shares, shares,
             pltpu.VMEM((8, 8, 64, NB), BF), pltpu.VMEM((8, 8, 64, NB), BF),
             pieces, pieces, pieces, pieces, pieces,
             pltpu.VMEM((2, NB, NB), F32), pltpu.VMEM((2, NB, NB), BF), pltpu.VMEM((2, NB, NB), BF),
             pltpu.VMEM((NB, NB), F32), pltpu.VMEM((2, 32, 128), I32), pltpu.VMEM((2, NB, 128), I32),
             pltpu.VMEM((NB, W), F32), pltpu.VMEM((NB, W), BF), pltpu.VMEM((NB, W), BF),
-            dma((8,)), dma((2,)), dma((8,)),
+            dma((8,)), dma((2,)),
             dma((8,)), dma((8,)), dma((8,)), dma((8,)), dma((8,)), dma((8,)), dma((2,)),
             dma((2, 8)), dma((2,)), dma((2, 4)), dma((2, 8)), dma((2, 8)),
-            dma((2, 2, 4)), dma((2, 2, 4)), dma((2, 2, 4)), dma((2, 2, 4)), dma((8,)), dma((8,)),
+            dma((2, 4, 4)), dma((2, 4, 4)), dma((2, 4, 4)), dma((2, 4, 4)), dma((8,)), dma((8,)),
         ],
         compiler_params=pltpu.CompilerParams(
             collective_id=0, has_side_effects=True, vmem_limit_bytes=60 << 20

time: 124 us -> 108 us (0.87)
  the two profiles are of different devices: /device:TPU:187 before, /device:TPU:32 now
where the time goes in v2:
time: 108 us
  Pallas kernels  106 us (98%)
  local copies, waits for them, and re-layouts  1.32 us (1%)
    pallas_call x1, Pallas kernels, on_device(): pl.pallas_call(kernel, out_shape=pltpu.VMEM(matrix.shape, matrix.dtype),...  106 us

profile of v2, /device:TPU:32, one launch (start us, length us, event | category | flops | bytes accessed | tf_op | source)
XLA Modules:
  0.0 107.8 jit_solution(13858578877304425457)
XLA Ops:
  0.0 106.5 %shard_map.46 = bf16[512,2048]{1,0:T(8,128)(2,1)S(1)} custom-call(bf16[512,2048]{1,0:T(8,128)(2,1)} %mat.1, s32[2,4096]{1,0:T(2,128)} %piv.1, f32[2,512,512]{2,1,0:T(8,128)} %low.1, f32[2,512,512]{2,1,0:T(8,128)} %upp.1), custom_call_target="tpu_custom_call" | custom-call | tf_op jit(solution)/shard_map/pallas_call | solution.py:435
  106.5 1.3 %copy.6 = bf16[512,2048]{1,0:T(8,128)(2,1)} copy(bf16[512,2048]{1,0:T(8,128)(2,1)S(1)} %shard_map.46) | data formatting | bytes 4194304

commit v3 on v2

--- a/solution.py
+++ b/solution.py
@@ -378,12 +378,21 @@
     forward(1, 2)
     update_again(0)
     forward(1, 3)
-    for s in range(1, 4):
-        update_again(s)
-
+    def send_if(wanted):
+        for d in PEERS:
+            q = peer(*d)
+
+            @pl.when(wanted(q // 2))
+            def _():
+                send_done(q).start()
+
+    send_if(lambda two: two == 0)
+    update_again(1)
+    update_again(2)
+    send_if(lambda two: two == pair(1) // 2)
+    update_again(3)
     out[:, mine] = fin[p]
-    for d in PEERS:
-        send_done(peer(*d)).start()
+    send_if(lambda two: (two != 0) & (two != pair(1) // 2))
 
     for d in PEERS:
         j = peer(*d)

time: 108 us -> 108 us (level)
  no operation moved by 1% of the time
where the time goes in v3:
time: 108 us
  Pallas kernels  106 us (98%)
  local copies, waits for them, and re-layouts  1.32 us (1%)
    pallas_call x1, Pallas kernels, on_device(): pl.pallas_call(kernel, out_shape=pltpu.VMEM(matrix.shape, matrix.dtype),...  106 us

profile of v3, /device:TPU:32, one launch (start us, length us, event | category | flops | bytes accessed | tf_op | source)
XLA Modules:
  0.0 107.7 jit_solution(2891795417228356176)
XLA Ops:
  0.0 106.4 %shard_map.46 = bf16[512,2048]{1,0:T(8,128)(2,1)S(1)} custom-call(bf16[512,2048]{1,0:T(8,128)(2,1)} %mat.1, s32[2,4096]{1,0:T(2,128)} %piv.1, f32[2,512,512]{2,1,0:T(8,128)} %low.1, f32[2,512,512]{2,1,0:T(8,128)} %upp.1), custom_call_target="tpu_custom_call" | custom-call | tf_op jit(solution)/shard_map/pallas_call | solution.py:444
  106.4 1.3 %copy.6 = bf16[512,2048]{1,0:T(8,128)(2,1)} copy(bf16[512,2048]{1,0:T(8,128)(2,1)S(1)} %shard_map.46) | data formatting | bytes 4194304
